TPU v7x, 512 devices: a whole 4x8x8 slice. The times are simulated.
512 devices in a mesh: tm: 16 (over y, core), vert: 32 (over x, z).
Axes of the slice: x: 4, y: 8, z: 8, core: 2. Of those that a mesh axis runs over, the one named last changes fastest.
Arguments:
- features: bfloat16 [16, 16384, 1024], P('tm', 'vert'), may hold values from -6 to 6
- graph_weight: bfloat16 [1024, 1024], P('vert'), may hold values from -0.1875 to 0.1875
- head_weight: bfloat16 [16, 192, 1024], P('tm'), may hold values from -16 to 16
- send_rows: int32 [16, 32, 32, 16], P('tm', 'vert'), may hold values from 0 to 511, as said below
- send_count: int32 [16, 32, 32], P('tm', 'vert'), may hold values from 0 to 16, as said below
- block_index: int32 [16, 128, 3], P('tm', 'vert'), may hold values from 0 to 7, as said below
- block_values: bfloat16 [16, 16384, 3, 128], P('tm', 'vert'), may hold values from -0.3125 to 0.3125
Outputs:
- combined: bfloat16 [16, 16384, 1024], P('tm', 'vert')
Inputs may be any that keep to these rules, and one draw needn't show every extreme that they name: send_rows[s, p, q] holds 16 distinct local rows of partition p; slots from send_count[s, p, q] on are ignored. send_count[s, p, p] is 0; in every snapshot some pairs reach 16. `block_index`: the 3 entries of a block row are distinct; column blocks below 4 are the partition's own rows, the others its boundary rows in the order of columns.
All inputs are finite; a program needn't handle non-finite values.
Results may differ from a plain program's by a relative error of at most 0.0075.
Values may be sent and summed in bfloat16 or wider, within the bound.
A program may use at most 64 MiB of HBM per device.

v0:
```python
import jax
import jax.numpy as jnp
from jax import lax
from jax.sharding import PartitionSpec as P


def attend_heads(regrouped, head_piece):
    head_size = head_piece.shape[1] // 3
    count_heads = head_piece.shape[0]
    snapshots = regrouped.shape[0]
    packed = jnp.einsum("tvd,hcd->tvhc", regrouped, head_piece, preferred_element_type=jnp.float32)
    queries = packed[..., :head_size].astype(jnp.bfloat16)
    keys_part = packed[..., head_size : 2 * head_size].astype(jnp.bfloat16)
    values = packed[..., 2 * head_size :].astype(jnp.bfloat16)
    scores = jnp.einsum(
        "tvhc,svhc->vhts", queries, keys_part, preferred_element_type=jnp.float32
    ) * head_size ** (-0.5)
    causal = jnp.arange(snapshots)[:, None] >= jnp.arange(snapshots)[None, :]
    scores = jnp.where(causal, scores, -1e30)
    row_max = jnp.max(scores, axis=-1, keepdims=True)
    exponent = jnp.where(causal, jnp.exp(scores - row_max), 0.0)
    attention = (exponent / jnp.sum(exponent, axis=-1, keepdims=True)).astype(jnp.bfloat16)
    attended = jnp.einsum("vhts,svhc->tvhc", attention, values, preferred_element_type=jnp.float32)
    return attended.astype(jnp.bfloat16).reshape(
        snapshots, regrouped.shape[1], count_heads * head_size
    )


def fold_rows(left, piece):
    return jnp.dot(left, piece, preferred_element_type=jnp.float32)


def shards(features, graph_weight, head_weight, send_rows, send_count, block_index, block_values):
    inputs = features[0]
    feature_width = inputs.shape[1]
    own_count = inputs.shape[0]
    rows_list = send_rows[0, 0]
    sources = rows_list.shape[0]
    most_rows = rows_list.shape[1]
    live_slots = jnp.arange(most_rows)[None, :] < send_count[0, 0][:, None]
    projected = fold_rows(inputs, lax.all_gather(graph_weight, "vert", axis=0, tiled=True)).astype(
        jnp.bfloat16
    )
    picked = jnp.take(projected, rows_list.reshape(-1), axis=0).reshape(
        sources, most_rows, feature_width
    )
    picked = jnp.where(live_slots[:, :, None], picked, jnp.zeros_like(picked))
    received = lax.all_to_all(picked, "vert", split_axis=0, concat_axis=0, tiled=True)
    block_size = block_values.shape[-1]
    index_list = block_index[0]
    own_blocks = index_list.shape[0]
    chosen_count = index_list.shape[1]
    columns = jnp.concatenate(
        [projected, received.reshape(sources * most_rows, feature_width)], axis=0
    )
    columns = columns.reshape(-1, block_size, feature_width)
    chosen = jnp.take(columns, index_list.reshape(-1), axis=0).reshape(
        own_blocks, chosen_count, block_size, feature_width
    )
    edge_weights = block_values[0].reshape(own_blocks, block_size, chosen_count, block_size)
    summed = jnp.einsum("rikj,rkjd->rid", edge_weights, chosen, preferred_element_type=jnp.float32)
    pre_act = projected.astype(jnp.float32) + summed.reshape(own_count, feature_width)
    hidden = jax.nn.relu(pre_act).astype(jnp.bfloat16)
    regrouped = lax.all_to_all(hidden[None], "tm", split_axis=1, concat_axis=0, tiled=True)
    attended = attend_heads(regrouped, lax.all_gather(head_weight, "tm", axis=0, tiled=True))
    returned = lax.all_to_all(attended, "tm", split_axis=0, concat_axis=1, tiled=True)
    combined = (hidden.astype(jnp.float32) + returned[0].astype(jnp.float32)).astype(jnp.bfloat16)
    return combined[None]


def solution(mesh):
    return jax.shard_map(
        shards,
        mesh=mesh,
        in_specs=(
            P("tm", "vert", None),
            P("vert", None),
            P("tm", None, None),
            P("tm", "vert", None, None),
            P("tm", "vert", None),
            P("tm", "vert", None),
            P("tm", "vert", None, None),
        ),
        out_specs=P("tm", "vert", None),
        check_vma=False,
    )
```

profile of v0, /device:TPU:1, one launch (start us, length us, event | category | flops | bytes accessed | tf_op | source)
XLA Modules:
  0.0 263.2 jit_solution(4501448001142894589)
XLA Ops:
  6.5 0.7 all-gather.3.cloned.1.call-update
  7.3 0.7 all-gather.5.cloned.1.call-update
  8.0 0.8 copy.39
  8.9 0.7 compare_and_fusion
  9.7 0.7 iota_compare_fusion
  10.4 84.7 %all-gather.3.cloned.1.call-done = bf16[1024,1024]{1,0:T(8,128)(2,1)} async-done(((bf16[32,1024]{1,0:T(8,128)(2,1)}), bf16[1024,1024]{1,0:T(8,128)(2,1)}) %all-gather.3.cloned.1.call-update) | async-done | bytes 2097168 | tf_op jit(solution)/shard_map/all_gather | solution.py:41
  95.1 2.8 %convolution_convert_fusion = bf16[512,1024]{1,0:T(8,128)(2,1)S(1)} fusion(bf16[1024,1024]{1,0:T(8,128)(2,1)} %all-gather.3.cloned.1.call-done, bf16[1,512,1024]{2,1,0:T(8,128)(2,1)S(1)} %copy-done), kind=kOutput, calls=%fused_computation.30 | convolution fusion | flops 1074266112 | bytes 4194304 | tf_op jit(solution)/shard_map/dot_general | solution.py:30
  97.9 2.1 gather_fusion
  100.0 1.2 select_select_fusion
  101.2 5.9 %all-to-all-start = ((bf16[32,16,1024]{2,1,0:T(8,128)(2,1)}), bf16[32,16,1024]{2,1,0:T(8,128)(2,1)S(1)}, u32[]{:S(2)}, u32[]{:S(2)}) async-start(bf16[32,16,1024]{2,1,0:T(8,128)(2,1)} %select_select_fusion), calls=%async_computation | async-start | bytes 2097152 | tf_op jit(solution)/shard_map/all_to_all | solution.py:48
  107.4 19.0 %all-to-all-done = bf16[32,16,1024]{2,1,0:T(8,128)(2,1)S(1)} async-done(((bf16[32,16,1024]{2,1,0:T(8,128)(2,1)}), bf16[32,16,1024]{2,1,0:T(8,128)(2,1)S(1)}, u32[]{:S(2)}, u32[]{:S(2)}) %all-to-all-start) | async-done | bytes 1048608 | tf_op jit(solution)/shard_map/all_to_all | solution.py:48
  126.4 1.5 pad_maximum_fusion
  127.9 4.2 %gather_fusion.1 = bf16[12,128,1024]{2,1,0:T(8,128)(2,1)} fusion(bf16[8,128,1024]{2,1,0:T(8,128)(2,1)} %bitcast.57, s32[1024]{0:T(1024)S(1)} %pad_clamp_fusion), kind=kCustom, calls=%fused_computation.1 | custom fusion | bytes 6291504 | tf_op jit(solution)/shard_map/jit(_take)/gather | solution.py:57
  132.1 2.8 %fusion.4 = f32[4,1024,128,1]{1,2,3,0:T(8,128)S(1)} fusion(bf16[4,3,128,1024]{3,2,1,0:T(8,128)(2,1)} %bitcast.63, pred[4,3]{1,0:T(4,128)(4,1)S(1)} %compare_and_fusion.1, bf16[4,128,3,128]{3,1,0,2:T(8,128)(2,1)S(1)} %bitcast.67), kind=kOutput, calls=%fused_computation.9 | convolution fusion | flops 404226048 | bytes 5636108 | tf_op jit(solution)/shard_map/rikj,rkjd->rid/dot_general | solution.py:61
  134.9 0.4 fusion.13
  135.3 3.0 %copy.63 = bf16[1,512,1024]{2,0,1:T(2,128)(2,1)} copy(bf16[1,512,1024]{2,1,0:T(8,128)(2,1)S(1)} %bitcast.58) | data formatting | bytes 2097152 | tf_op jit(solution)/shard_map/broadcast_in_dim | solution.py:64
  138.3 0.5 broadcast.92
  138.8 8.1 %reduce = bf16[512,1024]{1,0:T(8,128)(2,1)S(1)} reduce(bf16[512,1,1024]{2,1,0:T(2,128)(2,1)} %bitcast.60, bf16[]{:T(256)} %broadcast.92), dimensions={1}, to_apply=%bitcast.56.reduce_sub_computation | reduce | bytes 2097154
  146.9 1.6 reshape.151
  148.5 16.7 %all-to-all-start.1 = ((bf16[16,2,16384]{2,1,0:T(2,128)(2,1)}), bf16[16,2,16384]{2,1,0:T(2,128)(2,1)S(1)}, u32[]{:S(2)}, u32[]{:S(2)}) async-start(bf16[16,2,16384]{2,1,0:T(2,128)(2,1)} %reshape.151), calls=%async_computation.1 | async-start | bytes 2097152 | tf_op jit(solution)/shard_map/all_to_all | solution.py:64
  165.2 28.0 %all-to-all-done.1 = bf16[16,2,16384]{2,1,0:T(2,128)(2,1)S(1)} async-done(((bf16[16,2,16384]{2,1,0:T(2,128)(2,1)}), bf16[16,2,16384]{2,1,0:T(2,128)(2,1)S(1)}, u32[]{:S(2)}, u32[]{:S(2)}) %all-to-all-start.1) | async-done | bytes 1048608 | tf_op jit(solution)/shard_map/all_to_all | solution.py:64
  193.2 3.5 %reshape.152 = bf16[512,1,1024]{2,1,0:T(2,128)(2,1)} reshape(bf16[16,2,16384]{2,1,0:T(2,128)(2,1)S(1)} %all-to-all-done.1) | data formatting | bytes 2097152
  196.7 2.0 copy.51
  198.7 7.5 %fusion.7 = bf16[16,32,16,192]{3,1,2,0:T(8,128)(2,1)S(1)} fusion(bf16[16,32,1024,1]{2,1,3,0:T(8,128)(2,1)S(1)} %bitcast.64, bf16[16,192,1024]{2,1,0:T(8,128)(2,1)} %all-gather.5.cloned.1.call-done), kind=kOutput, calls=%fused_computation.12 | convolution fusion | flops 3222798336 | bytes 10485760 | tf_op jit(solution)/shard_map/tvd,hcd->tvhc/dot_general | solution.py:11
  206.3 1.8 fusion.32
  208.1 4.7 %fusion.15 = f32[32,16,16,16]{2,3,1,0:T(8,128)S(1)} fusion(bf16[16,32,16,64]{3,1,2,0:T(8,128)(2,1)S(1)} %get-tuple-element.6, bf16[16,32,16,64]{3,1,2,0:T(8,128)(2,1)S(1)} %get-tuple-element.7), kind=kOutput, calls=%fused_computation.21 | convolution fusion | flops 16777216 | bytes 2621440 | tf_op jit(solution)/shard_map/tvhc,svhc->vhts/dot_general | solution.py:15
  212.7 2.1 fusion.33
  214.8 3.2 %convert_bitcast_fusion = bf16[16,32,16,64]{3,0,2,1:T(8,128)(2,1)S(1)} fusion(f32[32,16,16,16]{2,3,1,0:T(8,128)S(1)} %get-tuple-element.9, f32[32,16,16]{2,1,0:T(8,128)S(1)} %get-tuple-element.8, bf16[16,32,16,64]{3,1,2,0:T(8,128)(2,1)S(1)} %get-tuple-element.5), kind=kOutput, calls=%fused_computation.24 | convolution fusion | flops 17563648 | bytes 2654208 | tf_op jit(solution)/shard_map/vhts,svhc->tvhc/dot_general | solution.py:23
  218.1 1.9 copy.47
  220.0 3.2 %reshape.129 = bf16[16,32,1024]{2,1,0:T(8,128)(2,1)S(1)} reshape(bf16[16,32,16,64]{3,2,1,0:T(8,128)(2,1)} %copy.47) | data formatting | bytes 2097152 | tf_op jit(solution)/shard_map/reshape | solution.py:24
  223.2 31.7 %all_to_all.26 = bf16[16,32,1024]{2,1,0:T(8,128)(2,1)S(1)} all-to-all(bf16[16,32,1024]{2,1,0:T(8,128)(2,1)S(1)} %reshape.129), channel_id=1, replica_groups=mesh['tm'=16,'vert'=32] {'tm'}, dimensions={0} | all-to-all | bytes 2097152 | tf_op jit(solution)/shard_map/all_to_all | solution.py:66
  254.9 1.4 fusion.25
  (19 shorter events, 0.5 us)
Async XLA Ops:
  6.5 88.6 %copy-start = (bf16[1,512,1024]{2,1,0:T(8,128)(2,1)S(1)}, bf16[1,512,1024]{2,1,0:T(8,128)(2,1)}, u32[]{:S(2)}) copy-start(bf16[1,512,1024]{2,1,0:T(8,128)(2,1)} %param.7) | copy-start | bytes 3145732
  6.5 88.5 %all-gather.3.cloned.1.call-start = ((), (), s32[]{:S(2)}) async-start(), calls=%async_computation.3 | async-start | bytes 2162688 | tf_op jit(solution)/shard_map/all_gather | solution.py:41
  7.3 191.5 %all-gather.5.cloned.1.call-start = ((), (), s32[]{:S(2)}) async-start(), calls=%async_computation.4 | async-start | bytes 6684672 | tf_op jit(solution)/shard_map/all_gather | solution.py:65
  100.0 7.1 %copy-start.1 = (s32[1,4,3]{1,0,2:T(1,128)S(1)}, s32[1,4,3]{1,0,2:T(1,128)}, u32[]{:S(2)}) copy-start(s32[1,4,3]{1,0,2:T(1,128)} %param.12) | copy-start | bytes 148
  101.2 25.2 %all-to-all-start = ((bf16[32,16,1024]{2,1,0:T(8,128)(2,1)}), bf16[32,16,1024]{2,1,0:T(8,128)(2,1)S(1)}, u32[]{:S(2)}, u32[]{:S(2)}) async-start(bf16[32,16,1024]{2,1,0:T(8,128)(2,1)} %select_select_fusion), calls=%async_computation | async-start | bytes 2097152 | tf_op jit(solution)/shard_map/all_to_all | solution.py:48
  127.9 4.2 %copy-start.2 = (bf16[1,512,3,128]{3,1,2,0:T(8,128)(2,1)S(1)}, bf16[1,512,3,128]{3,1,2,0:T(8,128)(2,1)}, u32[]{:S(2)}) copy-start(bf16[1,512,3,128]{3,1,2,0:T(8,128)(2,1)} %param.13) | copy-start | bytes 1179652
  148.5 44.7 %all-to-all-start.1 = ((bf16[16,2,16384]{2,1,0:T(2,128)(2,1)}), bf16[16,2,16384]{2,1,0:T(2,128)(2,1)S(1)}, u32[]{:S(2)}, u32[]{:S(2)}) async-start(bf16[16,2,16384]{2,1,0:T(2,128)(2,1)} %reshape.151), calls=%async_computation.1 | async-start | bytes 2097152 | tf_op jit(solution)/shard_map/all_to_all | solution.py:64
Sparse Core Ops, SparseCore 0:
  10.5 84.5 all-gather.2
  97.2 50.5 all-gather.4
where the time goes:
time: 264 us; the launch traced here: 263 us
  waiting for transfers between devices  133 us (50%)
  blocking collectives  31.7 us (12%)
  local copies, waits for them, and re-layouts  24.9 us (9%)
  starting transfers between devices  22.7 us (9%)
  matrix products  21 us (8%)
  other arithmetic  16.2 us (6%)
  between operations  13.5 us (5%)
    all_gather x1, waiting for transfers between devices, shards(): lax.all_gather(graph_weight, 'vert', axis=0, tiled=True)  84.7 us
    all_to_all x1, blocking collectives, shards(): lax.all_to_all(attended, 'tm', split_axis=0, concat_axis=1, tiled=True)  31.7 us
    all_to_all x1, waiting for transfers between devices, shards(): lax.all_to_all(hidden[None], 'tm', split_axis=1, concat_axis=0, tiled=True)  28 us
    all_to_all x1, waiting for transfers between devices, shards(): lax.all_to_all(picked, 'vert', split_axis=0, concat_axis=0, tiled=True)  19 us
    all_to_all x1, starting transfers between devices, shards(): lax.all_to_all(hidden[None], 'tm', split_axis=1, concat_axis=0, tiled=True)  16.7 us
    unnamed x12, local copies, waits for them, and re-layouts  8.44 us
    unnamed x1, other arithmetic  8.09 us
    dot_general x1, matrix products, attend_heads(): jnp.einsum('tvd,hcd->tvhc', regrouped, head_piece, preferred_element_type...  7.53 us
  transfers between devices with their start and end apart: 4, of which 3 were waited for; matrix products, arithmetic and copies ran while one was open for 14% of the time, Pallas kernels for 0%

commit v1 on v0

--- a/solution.py
+++ b/solution.py
@@ -2,6 +2,13 @@
 import jax.numpy as jnp
 from jax import lax
 from jax.sharding import PartitionSpec as P
+
+
+def exchange_blocks(x, axis, split, join):
+    size = lax.axis_size(axis)
+    parts = jnp.stack(jnp.split(x, size, axis=split), axis=0)
+    parts = lax.all_to_all(parts, axis, split_axis=0, concat_axis=0)
+    return jnp.concatenate(parts, axis=join)
 
 
 def attend_heads(regrouped, head_piece):
@@ -61,7 +68,7 @@
     summed = jnp.einsum("rikj,rkjd->rid", edge_weights, chosen, preferred_element_type=jnp.float32)
     pre_act = projected.astype(jnp.float32) + summed.reshape(own_count, feature_width)
     hidden = jax.nn.relu(pre_act).astype(jnp.bfloat16)
-    regrouped = lax.all_to_all(hidden[None], "tm", split_axis=1, concat_axis=0, tiled=True)
+    regrouped = exchange_blocks(hidden[None], "tm", 1, 0)
     attended = attend_heads(regrouped, lax.all_gather(head_weight, "tm", axis=0, tiled=True))
     returned = lax.all_to_all(attended, "tm", split_axis=0, concat_axis=1, tiled=True)
     combined = (hidden.astype(jnp.float32) + returned[0].astype(jnp.float32)).astype(jnp.bfloat16)

time: 264 us -> 255 us (0.966)
  other arithmetic: 16.2 us -> 8.1 us
    unnamed x1 -> x0, other arithmetic: 8.09 us -> none
    broadcast_in_dim x1 -> x0, local copies, waits for them, and re-layouts: 2.96 us -> none  [shards(): hidden[None]]
    unnamed x12 -> x23, local copies, waits for them, and re-layouts: 8.44 us -> 10.4 us
  transfers between devices with their start and end apart: 4 -> 4, of which waited for: 3 -> 3; matrix products, arithmetic and copies ran while one was open for 14% -> 11% of each run, Pallas kernels for 0% -> 0%
where the time goes in v1:
time: 255 us
  waiting for transfers between devices  133 us (52%)
  blocking collectives  31.7 us (12%)
  local copies, waits for them, and re-layouts  24.5 us (10%)
  starting transfers between devices  22.6 us (9%)
  matrix products  21 us (8%)
  between operations  13.5 us (5%)
  other arithmetic  8.1 us (3%)
    all_gather x1, waiting for transfers between devices, shards(): lax.all_gather(graph_weight, 'vert', axis=0, tiled=True)  84.7 us
    all_to_all x1, blocking collectives, shards(): lax.all_to_all(attended, 'tm', split_axis=0, concat_axis=1, tiled=True)  31.7 us
    all_to_all x1, waiting for transfers between devices, exchange_blocks(): parts = lax.all_to_all(parts, axis, split_axis=0, concat_axis=0)  28 us
    all_to_all x1, waiting for transfers between devices, shards(): lax.all_to_all(picked, 'vert', split_axis=0, concat_axis=0, tiled=True)  19.2 us
    all_to_all x1, starting transfers between devices, exchange_blocks(): parts = lax.all_to_all(parts, axis, split_axis=0, concat_axis=0)  16.8 us
    unnamed x23, local copies, waits for them, and re-layouts  10.4 us
    dot_general x1, matrix products, attend_heads(): jnp.einsum('tvd,hcd->tvhc', regrouped, head_piece, preferred_element_type...  7.51 us
    all_to_all x1, starting transfers between devices, shards(): lax.all_to_all(picked, 'vert', split_axis=0, concat_axis=0, tiled=True)  5.74 us
  transfers between devices with their start and end apart: 4, of which 3 were waited for; matrix products, arithmetic and copies ran while one was open for 11% of the time, Pallas kernels for 0%

profile of v1, /device:TPU:1, one launch (start us, length us, event | category | flops | bytes accessed | tf_op | source)
XLA Modules:
  0.0 254.6 jit_solution(89406956544368100)
XLA Ops:
  6.5 0.7 all-gather.3.cloned.1.call-update
  7.3 0.7 all-gather.5.cloned.1.call-update
  8.0 0.8 copy.28
  8.9 0.7 compare_and_fusion
  9.7 0.7 iota_compare_fusion
  10.4 84.7 %all-gather.3.cloned.1.call-done = bf16[1024,1024]{1,0:T(8,128)(2,1)} async-done(((bf16[32,1024]{1,0:T(8,128)(2,1)}), bf16[1024,1024]{1,0:T(8,128)(2,1)}) %all-gather.3.cloned.1.call-update) | async-done | bytes 2097168 | tf_op jit(solution)/shard_map/all_gather | solution.py:48
  95.1 2.8 %convolution_convert_fusion = bf16[512,1024]{1,0:T(8,128)(2,1)S(1)} fusion(bf16[1024,1024]{1,0:T(8,128)(2,1)} %all-gather.3.cloned.1.call-done, bf16[1,512,1024]{2,1,0:T(8,128)(2,1)S(1)} %copy-done), kind=kOutput, calls=%fused_computation.30 | convolution fusion | flops 1074266112 | bytes 4194304 | tf_op jit(solution)/shard_map/dot_general | solution.py:37
  97.9 2.1 gather_fusion
  100.0 1.2 select_select_fusion
  101.2 5.7 %all-to-all-start = ((bf16[32,16,1024]{2,1,0:T(8,128)(2,1)}), bf16[32,16,1024]{2,1,0:T(8,128)(2,1)S(1)}, u32[]{:S(2)}, u32[]{:S(2)}) async-start(bf16[32,16,1024]{2,1,0:T(8,128)(2,1)} %select_select_fusion), calls=%async_computation | async-start | bytes 2097152 | tf_op jit(solution)/shard_map/all_to_all | solution.py:55
  107.2 19.2 %all-to-all-done = bf16[32,16,1024]{2,1,0:T(8,128)(2,1)S(1)} async-done(((bf16[32,16,1024]{2,1,0:T(8,128)(2,1)}), bf16[32,16,1024]{2,1,0:T(8,128)(2,1)S(1)}, u32[]{:S(2)}, u32[]{:S(2)}) %all-to-all-start) | async-done | bytes 1048608 | tf_op jit(solution)/shard_map/all_to_all | solution.py:55
  126.4 1.5 pad_maximum_fusion
  127.9 4.2 %gather_fusion.1 = bf16[12,128,1024]{2,1,0:T(8,128)(2,1)} fusion(bf16[8,128,1024]{2,1,0:T(8,128)(2,1)} %bitcast.119, s32[1024]{0:T(1024)S(1)} %pad_clamp_fusion), kind=kCustom, calls=%fused_computation.1 | custom fusion | bytes 6291504 | tf_op jit(solution)/shard_map/jit(_take)/gather | solution.py:64
  132.1 2.8 %fusion.4 = f32[4,1024,128,1]{1,2,3,0:T(8,128)S(1)} fusion(bf16[4,3,128,1024]{3,2,1,0:T(8,128)(2,1)} %bitcast.138, pred[4,3]{1,0:T(4,128)(4,1)S(1)} %compare_and_fusion.1, bf16[4,128,3,128]{3,1,0,2:T(8,128)(2,1)S(1)} %bitcast.141), kind=kOutput, calls=%fused_computation.9 | convolution fusion | flops 404226048 | bytes 5636108 | tf_op jit(solution)/shard_map/rikj,rkjd->rid/dot_general | solution.py:68
  135.3 0.6 fusion.44
  136.0 0.6 fusion.43
  136.6 0.6 fusion.42
  137.2 0.6 fusion.41
  137.9 0.6 fusion.40
  138.5 0.6 fusion.39
  139.8 0.6 fusion.37
  145.5 16.8 %all-to-all-start.1 = ((bf16[16,1,32,1024]{3,2,1,0:T(8,128)(2,1)}), bf16[16,1,32,1024]{3,2,1,0:T(8,128)(2,1)S(1)}, u32[]{:S(2)}, u32[]{:S(2)}) async-start(bf16[16,1,32,1024]{3,2,1,0:T(8,128)(2,1)} %fusion.29), calls=%async_computation.1 | async-start | bytes 2097152 | tf_op jit(solution)/shard_map/all_to_all | solution.py:10
  162.3 28.0 %all-to-all-done.1 = bf16[16,1,32,1024]{3,2,1,0:T(8,128)(2,1)S(1)} async-done(((bf16[16,1,32,1024]{3,2,1,0:T(8,128)(2,1)}), bf16[16,1,32,1024]{3,2,1,0:T(8,128)(2,1)S(1)}, u32[]{:S(2)}, u32[]{:S(2)}) %all-to-all-start.1) | async-done | bytes 1048608 | tf_op jit(solution)/shard_map/all_to_all | solution.py:10
  190.3 7.5 %fusion.7 = bf16[16,32,16,192]{3,1,2,0:T(8,128)(2,1)S(1)} fusion(bf16[16,192,1024]{2,1,0:T(8,128)(2,1)} %all-gather.5.cloned.1.call-done, bf16[16,1,32,1024]{3,2,1,0:T(8,128)(2,1)S(1)} %all-to-all-done.1), kind=kOutput, calls=%fused_computation.12 | convolution fusion | flops 3222798336 | bytes 10485760 | tf_op jit(solution)/shard_map/tvd,hcd->tvhc/dot_general | solution.py:18
  197.8 1.8 fusion.49
  199.6 4.7 %fusion.15 = f32[32,16,16,16]{2,3,1,0:T(8,128)S(1)} fusion(bf16[16,32,16,64]{3,1,2,0:T(8,128)(2,1)S(1)} %get-tuple-element.6, bf16[16,32,16,64]{3,1,2,0:T(8,128)(2,1)S(1)} %get-tuple-element.7), kind=kOutput, calls=%fused_computation.21 | convolution fusion | flops 16777216 | bytes 2621440 | tf_op jit(solution)/shard_map/tvhc,svhc->vhts/dot_general | solution.py:22
  204.2 2.1 fusion.50
  206.4 3.2 %convert_bitcast_fusion = bf16[16,32,16,64]{3,0,2,1:T(8,128)(2,1)S(1)} fusion(f32[32,16,16,16]{2,3,1,0:T(8,128)S(1)} %get-tuple-element.9, f32[32,16,16]{2,1,0:T(8,128)S(1)} %get-tuple-element.8, bf16[16,32,16,64]{3,1,2,0:T(8,128)(2,1)S(1)} %get-tuple-element.5), kind=kOutput, calls=%fused_computation.24 | convolution fusion | flops 17563648 | bytes 2654208 | tf_op jit(solution)/shard_map/vhts,svhc->tvhc/dot_general | solution.py:30
  209.6 1.9 copy.35
  211.5 3.2 %reshape.130 = bf16[16,32,1024]{2,1,0:T(8,128)(2,1)S(1)} reshape(bf16[16,32,16,64]{3,2,1,0:T(8,128)(2,1)} %copy.35) | data formatting | bytes 2097152 | tf_op jit(solution)/shard_map/reshape | solution.py:31
  214.7 31.7 %all_to_all.19 = bf16[16,32,1024]{2,1,0:T(8,128)(2,1)S(1)} all-to-all(bf16[16,32,1024]{2,1,0:T(8,128)(2,1)S(1)} %reshape.130), channel_id=1, replica_groups=mesh['tm'=16,'vert'=32] {'tm'}, dimensions={0} | all-to-all | bytes 2097152 | tf_op jit(solution)/shard_map/all_to_all | solution.py:73
  246.4 1.4 fusion.25
  (29 shorter events, 6.6 us)
Async XLA Ops:
  6.5 88.6 %copy-start = (bf16[1,512,1024]{2,1,0:T(8,128)(2,1)S(1)}, bf16[1,512,1024]{2,1,0:T(8,128)(2,1)}, u32[]{:S(2)}) copy-start(bf16[1,512,1024]{2,1,0:T(8,128)(2,1)} %param.7) | copy-start | bytes 3145732
  6.5 88.5 %all-gather.3.cloned.1.call-start = ((), (), s32[]{:S(2)}) async-start(), calls=%async_computation.3 | async-start | bytes 2162688 | tf_op jit(solution)/shard_map/all_gather | solution.py:48
  7.3 183.0 %all-gather.5.cloned.1.call-start = ((), (), s32[]{:S(2)}) async-start(), calls=%async_computation.4 | async-start | bytes 6684672 | tf_op jit(solution)/shard_map/all_gather | solution.py:72
  100.0 7.0 %copy-start.1 = (s32[1,4,3]{1,0,2:T(1,128)S(1)}, s32[1,4,3]{1,0,2:T(1,128)}, u32[]{:S(2)}) copy-start(s32[1,4,3]{1,0,2:T(1,128)} %param.12) | copy-start | bytes 148
  101.2 25.2 %all-to-all-start = ((bf16[32,16,1024]{2,1,0:T(8,128)(2,1)}), bf16[32,16,1024]{2,1,0:T(8,128)(2,1)S(1)}, u32[]{:S(2)}, u32[]{:S(2)}) async-start(bf16[32,16,1024]{2,1,0:T(8,128)(2,1)} %select_select_fusion), calls=%async_computation | async-start | bytes 2097152 | tf_op jit(solution)/shard_map/all_to_all | solution.py:55
  127.9 4.2 %copy-start.2 = (bf16[1,512,3,128]{3,1,2,0:T(8,128)(2,1)S(1)}, bf16[1,512,3,128]{3,1,2,0:T(8,128)(2,1)}, u32[]{:S(2)}) copy-start(bf16[1,512,3,128]{3,1,2,0:T(8,128)(2,1)} %param.13) | copy-start | bytes 1179652
  145.5 44.8 %all-to-all-start.1 = ((bf16[16,1,32,1024]{3,2,1,0:T(8,128)(2,1)}), bf16[16,1,32,1024]{3,2,1,0:T(8,128)(2,1)S(1)}, u32[]{:S(2)}, u32[]{:S(2)}) async-start(bf16[16,1,32,1024]{3,2,1,0:T(8,128)(2,1)} %fusion.29), calls=%async_computation.1 | async-start | bytes 2097152 | tf_op jit(solution)/shard_map/all_to_all | solution.py:10
Sparse Core Ops, SparseCore 0:
  10.5 84.5 all-gather.2
  97.2 50.5 all-gather.4
